TPU v7x, 32 devices: a whole 2x2x4 slice. The times are simulated.
32 devices in a mesh: depth: 2 (over core), rows: 2 (over x), shots: 8 (over z, y).
Axes of the slice: x: 2, y: 2, z: 4, core: 2. Of those that a mesh axis runs over, the one named last changes fastest.
Arguments:
- sources: float32 [2, 2, 1024, 1024], P('depth', None, 'rows', 'shots'), may hold values from -6 to 6
- factor: float32 [2, 2, 1024, 1024], P('depth', None, ('rows', 'shots')), may hold values from -0.09375 to 0.09375
- block_mask: int32 [2, 2, 8, 8], P('depth'), may hold values 0 or 1
- inverse_diagonal: float32 [2, 2, 1024, 1024], P('depth', None, None, 'rows'), may hold values from -1.2 to 1.2, as said below
Outputs:
- solution: float32 [2, 2, 1024, 1024], P('depth', None, 'rows', 'shots')
Inputs may be any that keep to these rules, and one draw needn't show every extreme that they name: Each block inverse_diagonal[d, m] is lower triangular with diagonal entries between 0.8 and 1.2.
All inputs are finite; a program needn't handle non-finite values. No bound on the sum of `block_mask` on one device may be relied on, other than what follows from the above.
Results may differ from a plain program's by a relative error of at most 0.0001.
Values sent between devices are 32-bit elements; how exact they have to be, the bound alone decides.
No kernel may reach another device: no remote copies, remote signals or barrier semaphores. Data moves between devices by JAX's collectives and lax.ppermute only.
A program may use at most 64 MiB of HBM per device.

v0:
```python
import jax
import jax.numpy as jnp
from jax import lax
from jax.sharding import PartitionSpec as P


def mask_rows(factor_rows, block_mask, row_start, block_size):
    row_total = factor_rows.shape[1]
    block_count = block_mask.shape[3]
    row_blocks = (row_start + jnp.arange(row_total, dtype=jnp.int32)) // block_size
    row_select = (row_blocks[:, None] == jnp.arange(block_count, dtype=jnp.int32)[None, :]).astype(
        jnp.float32
    )
    row_masks = jnp.einsum("rk,pkc->prc", row_select, block_mask[0].astype(jnp.float32))
    return factor_rows * jnp.repeat(row_masks, block_size, axis=2)


def group_reduce(partial_value):
    summed = lax.psum_scatter(partial_value, "depth", scatter_dimension=0, tiled=True)
    return summed[0]


def group_collect(spread):
    every_rows = lax.all_gather(spread[None], "depth", axis=0, tiled=True)
    return every_rows


def invert_level(inverse_block, own_rows):
    inverse_term = jnp.dot(
        inverse_block, own_rows, precision=lax.Precision.HIGHEST, preferred_element_type=jnp.float32
    )
    return lax.psum(inverse_term, "rows")


def per_device(sources, factor, block_mask, inverse_diagonal):
    depth_count = lax.axis_size("depth")
    tree_height = depth_count.bit_length() - 1
    level_count = tree_height + 1
    rows_index = lax.axis_index("rows")
    full_width = factor.shape[3]
    block_count = block_mask.shape[3]
    block_size = full_width // block_count
    highest = lax.Precision.HIGHEST
    front_factor = lax.all_gather(factor[0], "shots", axis=1, tiled=True)
    front_count = front_factor.shape[1]
    masked = mask_rows(front_factor, block_mask, rows_index * front_count, block_size)
    solved = []
    for tier_index in range(level_count):
        own_rows = sources[0, tier_index]
        if tier_index > 0:
            group_size = 2**tier_index
            factor_tiles = masked.reshape(tier_index, group_size, front_count, full_width)
            lower_solved = jnp.stack(solved[:tier_index])
            partial_value = jnp.einsum(
                "lgrs,lsn->grn",
                factor_tiles,
                lower_solved,
                precision=highest,
                preferred_element_type=jnp.float32,
            )
            reduced = group_reduce(partial_value)
            own_rows = own_rows - reduced
        full_rows = invert_level(inverse_diagonal[0, tier_index], own_rows)
        solved.append(full_rows)
    answers = [None] * level_count
    collected = {}
    for tier_index in reversed(range(level_count)):
        target = solved[tier_index]
        if tier_index < tree_height:
            factor_tiles = masked
            transposed = jnp.einsum(
                "grs,grn->sn",
                factor_tiles,
                collected[1],
                precision=highest,
                preferred_element_type=jnp.float32,
            )
            own_columns = lax.psum(transposed, "rows")
            target = target - own_columns
        answer = lax.dot_general(
            inverse_diagonal[0, tier_index],
            target,
            (((0,), (0,)), ((), ())),
            precision=highest,
            preferred_element_type=jnp.float32,
        )
        answers[tier_index] = answer
        if tier_index > 0:
            collected[tier_index] = group_collect(answer)
    return jnp.stack(answers)[None]


def solution(mesh):
    placed = (
        P("depth", None, "rows", "shots"),
        P("depth", None, ("rows", "shots"), None),
        P("depth", None, None, None),
        P("depth", None, None, "rows"),
    )
    return jax.shard_map(
        per_device,
        mesh=mesh,
        in_specs=placed,
        out_specs=P("depth", None, "rows", "shots"),
        check_vma=False,
    )
```

profile of v0, /device:TPU:0, one launch (start us, length us, event | category | flops | bytes accessed | tf_op | source)
XLA Modules:
  0.0 194.4 jit_solution(14296305653696996673)
XLA Ops:
  7.4 0.0 all-reduce.4.cloned.1.call-start
  7.4 4.2 %fusion.6 = f32[1024,128]{1,0:T(8,128)} fusion(f32[1,2,1024,512]{3,2,1,0:T(8,128)} %param.7, f32[1,2,512,128]{3,2,1,0:T(8,128)} %param.4), kind=kOutput, calls=%fused_computation.7 | convolution fusion | flops 805306368 | bytes 2883584 | tf_op jit(solution)/shard_map/dot_general | solution.py:29
  11.5 0.0 all-reduce.4.cloned.1.call-update
  11.6 0.0 all-gather.4.cloned.1.call-start
  11.6 0.5 all-gather.4.cloned.1.call-update
  12.2 0.0 reduce-scatter.2.cloned.1.call-start
  12.2 0.7 convert_bitcast_fusion
  12.9 0.1 copy.5
  13.0 0.1 convolution_bitcast_fusion
  13.1 0.2 copy.6
  13.3 2.6 %broadcast_in_dim.11 = f32[2,512,8,128]{3,2,1,0:T(8,128)} broadcast(f32[2,512,8]{2,1,0:T(8,128)S(1)} %copy.6), dimensions={0,1,2} | broadcast | bytes 4227072 | tf_op jit(solution)/shard_map/broadcast_in_dim | solution.py:15
  15.9 4.9 %reshape.30 = f32[2,512,1024]{2,1,0:T(8,128)} reshape(f32[2,512,8,128]{3,2,1,0:T(8,128)} %broadcast_in_dim.11) | data formatting | bytes 8388608 | tf_op jit(solution)/shard_map/reshape | solution.py:15
  20.8 0.0 copy-start.1
  20.8 22.3 %all-reduce.4.cloned.1.call-done = f32[1024,128]{1,0:T(8,128)} async-done(((f32[1024,128]{1,0:T(8,128)}), f32[1024,128]{1,0:T(8,128)}) %all-reduce.4.cloned.1.call-update) | async-done | bytes 524304 | tf_op jit(solution)/shard_map/psum | solution.py:32
  43.1 46.4 %all-gather.4.cloned.1.call-done = f32[1,2,512,1024]{3,2,1,0:T(8,128)} async-done(((f32[1,2,64,1024]{3,2,1,0:T(8,128)}), f32[1,2,512,1024]{3,2,1,0:T(8,128)}) %all-gather.4.cloned.1.call-update) | async-done | bytes 4194320 | tf_op jit(solution)/shard_map/all_gather | solution.py:44
  89.5 7.7 %fusion.13 = f32[2,512,128]{2,1,0:T(8,128)} fusion(f32[2,512,1024]{2,1,0:T(8,128)} %reshape.30, f32[1,2,512,1024]{3,2,1,0:T(8,128)} %all-gather.4.cloned.1.call-done, f32[1024,128]{1,0:T(8,128)} %all-reduce.4.cloned.1.call-done), kind=kOutput, calls=%fused_computation.14 | convolution fusion | flops 1611661312 | bytes 9437184 | tf_op jit(solution)/shard_map/lgrs,lsn->grn/dot_general | solution.py:54
  97.2 0.0 reduce-scatter.2.cloned.1.call-update
  97.3 0.0 all-reduce.6.cloned.1.call-start
  97.3 6.6 %reduce-scatter.2.cloned.1.call-done = f32[1,512,128]{2,1,0:T(8,128)} async-done(((f32[2,512,128]{2,1,0:T(8,128)}), f32[1,512,128]{2,1,0:T(8,128)}) %reduce-scatter.2.cloned.1.call-update) | async-done | bytes 262160 | tf_op jit(solution)/shard_map/reduce_scatter | solution.py:19
  103.9 0.0 copy-done.1
  103.9 4.8 %fusion.15 = f32[1024,128]{0,1:T(8,128)} fusion(f32[1,2,1024,512]{3,2,1,0:T(8,128)} %param.7, f32[1,512,128]{2,1,0:T(8,128)} %reduce-scatter.2.cloned.1.call-done, f32[1,2,512,128]{3,2,1,0:T(8,128)S(1)} %copy-done.1), kind=kOutput, calls=%fused_computation.16 | convolution fusion | flops 805371904 | bytes 3145728 | tf_op jit(solution)/shard_map/dot_general | solution.py:29
  108.7 0.0 all-reduce.6.cloned.1.call-update
  108.7 0.0 all-reduce.8.cloned.1.call-start
  108.8 29.9 %all-reduce.6.cloned.1.call-done = f32[1024,128]{0,1:T(8,128)} async-done(((f32[1024,128]{0,1:T(8,128)}), f32[1024,128]{0,1:T(8,128)}) %all-reduce.6.cloned.1.call-update) | async-done | bytes 524304 | tf_op jit(solution)/shard_map/psum | solution.py:32
  138.7 3.1 %fusion = f32[128,512]{1,0:T(8,128)S(1)} fusion(f32[1024,128]{0,1:T(8,128)} %all-reduce.6.cloned.1.call-done, f32[1,2,1024,512]{3,2,1,0:T(8,128)} %param.7), kind=kOutput, calls=%fused_computation.1 | convolution fusion | flops 805306368 | bytes 2883584 | tf_op jit(solution)/shard_map/dot_general | solution.py:80
  141.7 2.4 %all-gather.1 = f32[1024,128]{0,1:T(8,128)S(1)} all-gather(f32[512,128]{0,1:T(8,128)S(1)} %bitcast.63), channel_id=3, replica_groups=mesh['depth'=2,'rows'=2,'shots'=8] {'depth'}, dimensions={0}, use_global_device_ids=true | all-gather | bytes 786432 | tf_op jit(solution)/shard_map/all_gather | solution.py:24
  144.1 0.2 copy.9
  144.3 0.0 copy-start
  144.3 10.0 %fusion.14 = f32[1024,128]{1,0:T(8,128)} fusion(f32[2,512,128]{2,1,0:T(8,128)S(1)} %bitcast.65, f32[2,512,1024]{2,1,0:T(8,128)} %reshape.30, f32[1,2,512,1024]{3,2,1,0:T(8,128)} %all-gather.4.cloned.1.call-done), kind=kOutput, calls=%fused_computation.15 | convolution fusion | flops 1611661312 | bytes 9437184 | tf_op jit(solution)/shard_map/grs,grn->sn/dot_general | solution.py:71
  154.3 0.0 all-reduce.8.cloned.1.call-update
  154.3 28.8 %all-reduce.8.cloned.1.call-done = f32[1024,128]{1,0:T(8,128)} async-done(((f32[1024,128]{1,0:T(8,128)}), f32[1024,128]{1,0:T(8,128)}) %all-reduce.8.cloned.1.call-update) | async-done | bytes 524304 | tf_op jit(solution)/shard_map/psum | solution.py:78
  183.1 0.0 copy-done
  183.1 3.2 %fusion.18 = f32[1,512,128]{1,2,0:T(8,128)S(1)} fusion(f32[1,2,1024,512]{3,2,1,0:T(8,128)} %param.7, f32[1024,128]{1,0:T(8,128)S(1)} %copy-done, f32[1024,128]{1,0:T(8,128)} %all-reduce.8.cloned.1.call-done), kind=kOutput, calls=%fused_computation.17 | convolution fusion | flops 805437440 | bytes 3407872 | tf_op jit(solution)/shard_map/dot_general | solution.py:80
  186.3 1.0 copy.7
  (2 shorter events, 0.0 us)
Async XLA Ops:
  7.4 35.7 %all-reduce.4.cloned.1.call-start = ((), (), s32[]{:S(2)}) async-start(), calls=%async_computation.1 | async-start | bytes 1048576 | tf_op jit(solution)/shard_map/psum | solution.py:32
  11.6 78.0 %all-gather.4.cloned.1.call-start = ((), (), s32[]{:S(2)}) async-start(), calls=%async_computation.5 | async-start | bytes 4718592 | tf_op jit(solution)/shard_map/all_gather | solution.py:44
  12.2 91.8 %reduce-scatter.2.cloned.1.call-start = ((), (), s32[]{:S(2)}) async-start(), calls=%async_computation.2 | async-start | bytes 786432 | tf_op jit(solution)/shard_map/reduce_scatter | solution.py:19
  20.8 83.1 %copy-start.1 = (f32[1,2,512,128]{3,2,1,0:T(8,128)S(1)}, f32[1,2,512,128]{3,2,1,0:T(8,128)}, u32[]{:S(2)}) copy-start(f32[1,2,512,128]{3,2,1,0:T(8,128)} %param.4) | copy-start | bytes 1572868
  97.3 41.4 %all-reduce.6.cloned.1.call-start = ((), (), s32[]{:S(2)}) async-start(), calls=%async_computation.3 | async-start | bytes 1048576 | tf_op jit(solution)/shard_map/psum | solution.py:32
  108.7 74.3 %all-reduce.8.cloned.1.call-start = ((), (), s32[]{:S(2)}) async-start(), calls=%async_computation.4 | async-start | bytes 1048576 | tf_op jit(solution)/shard_map/psum | solution.py:78
  144.3 38.8 %copy-start = (f32[1024,128]{1,0:T(8,128)S(1)}, f32[1024,128]{1,0:T(8,128)}, u32[]{:S(2)}) copy-start(f32[1024,128]{1,0:T(8,128)} %all-reduce.4.cloned.1.call-done) | copy-start | bytes 1572868
Sparse Core Ops, SparseCore 0:
  11.7 31.3 all-reduce.3
  97.4 6.5 reduce-scatter.1
  108.9 29.7 all-reduce.5
  154.4 28.6 all-reduce.7
Sparse Core Ops, SparseCore 1:
  14.2 75.2 all-gather.3
where the time goes:
time: 195 us; the launch traced here: 194 us
  waiting for transfers between devices  135 us (69%)
  matrix products  33 us (17%)
  between operations  14.6 us (7%)
  local copies, waits for them, and re-layouts  8.97 us (5%)
  blocking collectives  2.36 us (1%)
    psum x2, waiting for transfers between devices, invert_level(): return lax.psum(inverse_term, 'rows')  52.1 us
    all_gather x1, waiting for transfers between devices, per_device(): front_factor = lax.all_gather(factor[0], 'shots', axis=1, tiled=True)  46.4 us
    psum x1, waiting for transfers between devices, per_device(): own_columns = lax.psum(transposed, 'rows')  28.8 us
    dot_general x1, matrix products, per_device(): jnp.einsum('grs,grn->sn', factor_tiles, collected[1], precision=highest,...  9.96 us
    dot_general x2, matrix products, invert_level(): jnp.dot(inverse_block, own_rows, precision=lax.Precision.HIGHEST, preferr...  8.97 us
    dot_general x1, matrix products, per_device(): jnp.einsum('lgrs,lsn->grn', factor_tiles, lower_solved, precision=highest...  7.7 us
    reduce_scatter x1, waiting for transfers between devices, group_reduce(): lax.psum_scatter(partial_value, 'depth', scatter_dimension=0, tiled=True)  6.63 us
    dot_general x2, matrix products, per_device(): lax.dot_general(inverse_diagonal[0, tier_index], target, (((0,), (0,)), (...  6.22 us
  transfers between devices with their start and end apart: 5, of which 5 were waited for; matrix products, arithmetic and copies ran while one was open for 4% of the time, Pallas kernels for 0%

commit v1 on v0

--- a/solution.py
+++ b/solution.py
@@ -41,7 +41,14 @@
     block_count = block_mask.shape[3]
     block_size = full_width // block_count
     highest = lax.Precision.HIGHEST
-    front_factor = lax.all_gather(factor[0], "shots", axis=1, tiled=True)
+    ring = [factor[0]]
+    for hop in range(7):
+        ring.append(lax.ppermute(ring[-1], "shots", [(dev, (dev + 1) % 8) for dev in range(8)]))
+    front_factor = jnp.roll(
+        jnp.concatenate(ring[::-1], axis=1),
+        (lax.axis_index("shots") + 1) * ring[0].shape[1],
+        axis=1,
+    )
     front_count = front_factor.shape[1]
     masked = mask_rows(front_factor, block_mask, rows_index * front_count, block_size)
     solved = []

time: 195 us -> 235 us (1.21)
  waiting for transfers between devices: 135 us -> 156 us
  local copies, waits for them, and re-layouts: 8.97 us -> 26.5 us
  starting transfers between devices: 0.17 us -> 3.14 us
    ppermute x0 -> x7, waiting for transfers between devices: none -> 85.6 us  [per_device(): lax.ppermute(ring[-1], 'shots', [(dev, (dev + 1) % 8) for dev in range(8)])]
    all_gather x1 -> x0, waiting for transfers between devices: 46.4 us -> none  [per_device(): front_factor = lax.all_gather(factor[0], 'shots', axis=1, tiled=True)]
    psum x2, waiting for transfers between devices: 52.1 us -> 33 us  [invert_level(): return lax.psum(inverse_term, 'rows')]
    unnamed x4 -> x21, local copies, waits for them, and re-layouts: 0.01 us -> 16.6 us
    ppermute x0 -> x7, starting transfers between devices: none -> 3.01 us  [per_device(): lax.ppermute(ring[-1], 'shots', [(dev, (dev + 1) % 8) for dev in range(8)])]
  transfers between devices with their start and end apart: 5 -> 11, of which waited for: 5 -> 10; matrix products, arithmetic and copies ran while one was open for 4% -> 13% of each run, Pallas kernels for 0% -> 0%
where the time goes in v1:
time: 235 us; the launch traced here: 234 us
  waiting for transfers between devices  156 us (66%)
  matrix products  32.9 us (14%)
  local copies, waits for them, and re-layouts  26.5 us (11%)
  between operations  13.2 us (6%)
  starting transfers between devices  3.14 us (1%)
  blocking collectives  2.36 us (1%)
    ppermute x7, waiting for transfers between devices, per_device(): lax.ppermute(ring[-1], 'shots', [(dev, (dev + 1) % 8) for dev in range(8)])  85.6 us
    psum x2, waiting for transfers between devices, invert_level(): return lax.psum(inverse_term, 'rows')  33 us
    psum x1, waiting for transfers between devices, per_device(): own_columns = lax.psum(transposed, 'rows')  28.8 us
    unnamed x21, local copies, waits for them, and re-layouts  16.6 us
    dot_general x1, matrix products, per_device(): jnp.einsum('grs,grn->sn', factor_tiles, collected[1], precision=highest,...  9.92 us
    dot_general x2, matrix products, invert_level(): jnp.dot(inverse_block, own_rows, precision=lax.Precision.HIGHEST, preferr...  8.97 us
    reduce_scatter x1, waiting for transfers between devices, group_reduce(): lax.psum_scatter(partial_value, 'depth', scatter_dimension=0, tiled=True)  8.03 us
    dot_general x1, matrix products, per_device(): jnp.einsum('lgrs,lsn->grn', factor_tiles, lower_solved, precision=highest...  7.7 us
  transfers between devices with their start and end apart: 11, of which 10 were waited for; matrix products, arithmetic and copies ran while one was open for 13% of the time, Pallas kernels for 0%

profile of v1, /device:TPU:0, one launch (start us, length us, event | category | flops | bytes accessed | tf_op | source)
XLA Modules:
  0.0 234.4 jit_solution(1825163214542470106)
XLA Ops:
  6.5 3.0 %collective-permute-start = (f32[2,64,1024]{2,1,0:T(8,128)}, f32[2,64,1024]{2,1,0:T(8,128)S(1)}, u32[]{:S(2)}, u32[]{:S(2)}) collective-permute-start(f32[2,64,1024]{2,1,0:T(8,128)} %bitcast.63), channel_id=1, source_target_pairs={{0,1},{1,2},{2,3},{3,4},{4,5},{5,6},{6,7},{7,0},{8,9},{9,10},{10,1... | collective-permute-start | bytes 1572872 | tf_op jit(solution)/shard_map/ppermute | solution.py:46
  9.5 15.2 %collective-permute-done = f32[2,64,1024]{2,1,0:T(8,128)S(1)} collective-permute-done((f32[2,64,1024]{2,1,0:T(8,128)}, f32[2,64,1024]{2,1,0:T(8,128)S(1)}, u32[]{:S(2)}, u32[]{:S(2)}) %collective-permute-start) | collective-permute-done | bytes 524320 | tf_op jit(solution)/shard_map/ppermute | solution.py:46
  24.7 15.8 %collective-permute-done.1 = f32[2,64,1024]{2,1,0:T(8,128)S(1)} collective-permute-done((f32[2,64,1024]{2,1,0:T(8,128)S(1)}, f32[2,64,1024]{2,1,0:T(8,128)S(1)}, u32[]{:S(2)}, u32[]{:S(2)}) %collective-permute-start.1) | collective-permute-done | bytes 524320 | tf_op jit(solution)/shard_map/ppermute | solution.py:46
  40.5 14.9 %collective-permute-done.2 = f32[2,64,1024]{2,1,0:T(8,128)S(1)} collective-permute-done((f32[2,64,1024]{2,1,0:T(8,128)S(1)}, f32[2,64,1024]{2,1,0:T(8,128)S(1)}, u32[]{:S(2)}, u32[]{:S(2)}) %collective-permute-start.2) | collective-permute-done | bytes 524320 | tf_op jit(solution)/shard_map/ppermute | solution.py:46
  55.4 14.1 %collective-permute-done.3 = f32[2,64,1024]{2,1,0:T(8,128)S(1)} collective-permute-done((f32[2,64,1024]{2,1,0:T(8,128)S(1)}, f32[2,64,1024]{2,1,0:T(8,128)S(1)}, u32[]{:S(2)}, u32[]{:S(2)}) %collective-permute-start.3) | collective-permute-done | bytes 524320 | tf_op jit(solution)/shard_map/ppermute | solution.py:46
  69.5 13.2 %collective-permute-done.4 = f32[2,64,1024]{2,1,0:T(8,128)S(1)} collective-permute-done((f32[2,64,1024]{2,1,0:T(8,128)S(1)}, f32[2,64,1024]{2,1,0:T(8,128)S(1)}, u32[]{:S(2)}, u32[]{:S(2)}) %collective-permute-start.4) | collective-permute-done | bytes 524320 | tf_op jit(solution)/shard_map/ppermute | solution.py:46
  82.7 12.5 %collective-permute-done.5 = f32[2,64,1024]{2,1,0:T(8,128)} collective-permute-done((f32[2,64,1024]{2,1,0:T(8,128)S(1)}, f32[2,64,1024]{2,1,0:T(8,128)}, u32[]{:S(2)}, u32[]{:S(2)}) %collective-permute-start.5) | collective-permute-done | bytes 524320 | tf_op jit(solution)/shard_map/ppermute | solution.py:46
  95.2 4.2 %fusion.6 = f32[1024,128]{1,0:T(8,128)} fusion(f32[1,2,1024,512]{3,2,1,0:T(8,128)} %param.7, f32[1,2,512,128]{3,2,1,0:T(8,128)} %param.4), kind=kOutput, calls=%fused_computation.7 | convolution fusion | flops 805306368 | bytes 2883584 | tf_op jit(solution)/shard_map/dot_general | solution.py:29
  99.4 0.0 reduce-scatter.2.cloned.1.call-start
  99.5 0.7 convert_bitcast_fusion
  100.2 0.1 copy.5
  100.3 0.1 convolution_bitcast_fusion
  100.4 0.2 copy.6
  100.6 2.6 %broadcast_in_dim.11 = f32[2,512,8,128]{3,2,1,0:T(8,128)} broadcast(f32[2,512,8]{2,1,0:T(8,128)S(1)} %copy.6), dimensions={0,1,2} | broadcast | bytes 4227072 | tf_op jit(solution)/shard_map/broadcast_in_dim | solution.py:15
  103.2 5.0 %reshape.30 = f32[2,512,1024]{2,1,0:T(8,128)} reshape(f32[2,512,8,128]{3,2,1,0:T(8,128)} %broadcast_in_dim.11) | data formatting | bytes 8388608 | tf_op jit(solution)/shard_map/reshape | solution.py:15
  108.2 1.9 constant_dynamic-update-slice_fusion.15
  110.0 1.9 constant_dynamic-update-slice_fusion.14
  111.9 0.8 constant_dynamic-update-slice_fusion.13
  112.7 0.8 constant_dynamic-update-slice_fusion.12
  113.6 0.8 constant_dynamic-update-slice_fusion.11
  114.4 0.8 constant_dynamic-update-slice_fusion.10
  115.2 0.8 constant_dynamic-update-slice_fusion.9
  116.1 0.8 constant_dynamic-update-slice_fusion.8
  116.9 1.9 constant_dynamic-update-slice_fusion.7
  118.7 1.9 constant_dynamic-update-slice_fusion.6
  120.6 0.8 constant_dynamic-update-slice_fusion.5
  121.5 0.8 constant_dynamic-update-slice_fusion.4
  122.3 0.8 constant_dynamic-update-slice_fusion.3
  123.1 0.8 constant_dynamic-update-slice_fusion.2
  123.9 0.8 constant_dynamic-update-slice_fusion.1
  124.7 0.9 constant_dynamic-update-slice_fusion
  125.6 3.1 %all-reduce.4.cloned.1.call-done = f32[1024,128]{1,0:T(8,128)} async-done(((f32[1024,128]{1,0:T(8,128)}), f32[1024,128]{1,0:T(8,128)}) %all-reduce.4.cloned.1.call-update) | async-done | bytes 524304 | tf_op jit(solution)/shard_map/psum | solution.py:32
  128.8 7.7 %fusion.13 = f32[2,512,128]{2,1,0:T(8,128)} fusion(f32[2,512,1024]{2,1,0:T(8,128)} %reshape.30, f32[2,1024,1024]{2,1,0:T(8,128)} %constant_dynamic-update-slice_fusion, s32[]{:T(128)S(6)} %select_n.23, f32[1024,128]{1,0:T(8,128)} %all-reduce.4.cloned.1.call-done), kind=kOutput, calls=%fused_computation.14 | convolution fusion | flops 1611661312 | bytes 9437188 | tf_op jit(solution)/shard_map/lgrs,lsn->grn/dot_general | solution.py:61
  136.5 0.0 reduce-scatter.2.cloned.1.call-update
  136.5 0.0 all-reduce.6.cloned.1.call-start
  136.5 8.0 %reduce-scatter.2.cloned.1.call-done = f32[1,512,128]{2,1,0:T(8,128)} async-done(((f32[2,512,128]{2,1,0:T(8,128)}), f32[1,512,128]{2,1,0:T(8,128)}) %reduce-scatter.2.cloned.1.call-update) | async-done | bytes 262160 | tf_op jit(solution)/shard_map/reduce_scatter | solution.py:19
  144.6 4.8 %fusion.14 = f32[1024,128]{0,1:T(8,128)} fusion(f32[1,2,1024,512]{3,2,1,0:T(8,128)} %param.7, f32[1,512,128]{2,1,0:T(8,128)} %reduce-scatter.2.cloned.1.call-done, f32[1,2,512,128]{3,2,1,0:T(8,128)S(1)} %copy-done.2), kind=kOutput, calls=%fused_computation.15 | convolution fusion | flops 805371904 | bytes 3145728 | tf_op jit(solution)/shard_map/dot_general | solution.py:29
  149.4 0.0 all-reduce.6.cloned.1.call-update
  149.4 0.0 all-reduce.8.cloned.1.call-start
  149.4 29.9 %all-reduce.6.cloned.1.call-done = f32[1024,128]{0,1:T(8,128)} async-done(((f32[1024,128]{0,1:T(8,128)}), f32[1024,128]{0,1:T(8,128)}) %all-reduce.6.cloned.1.call-update) | async-done | bytes 524304 | tf_op jit(solution)/shard_map/psum | solution.py:32
  179.3 3.1 %fusion = f32[128,512]{1,0:T(8,128)S(1)} fusion(f32[1024,128]{0,1:T(8,128)} %all-reduce.6.cloned.1.call-done, f32[1,2,1024,512]{3,2,1,0:T(8,128)} %param.7), kind=kOutput, calls=%fused_computation.1 | convolution fusion | flops 805306368 | bytes 2883584 | tf_op jit(solution)/shard_map/dot_general | solution.py:87
  182.4 2.4 %all-gather = f32[1024,128]{0,1:T(8,128)S(1)} all-gather(f32[512,128]{0,1:T(8,128)S(1)} %bitcast.60), channel_id=2, replica_groups=mesh['depth'=2,'rows'=2,'shots'=8] {'depth'}, dimensions={0}, use_global_device_ids=true | all-gather | bytes 786432 | tf_op jit(solution)/shard_map/all_gather | solution.py:24
  184.7 0.2 copy.9
  184.9 9.9 %fusion.17 = f32[1024,128]{1,0:T(8,128)} fusion(f32[2,512,128]{2,1,0:T(8,128)S(1)} %bitcast.62, f32[2,512,1024]{2,1,0:T(8,128)} %reshape.30, f32[2,1024,1024]{2,1,0:T(8,128)} %constant_dynamic-update-slice_fusion, s32[]{:T(128)S(6)} %select_n.23), kind=kOutput, calls=%fused_computation.16 | convolution fusion | flops 1611661312 | bytes 9437188 | tf_op jit(solution)/shard_map/grs,grn->sn/dot_general | solution.py:78
  194.8 0.0 all-reduce.8.cloned.1.call-update
  194.9 28.8 %all-reduce.8.cloned.1.call-done = f32[1024,128]{1,0:T(8,128)} async-done(((f32[1024,128]{1,0:T(8,128)}), f32[1024,128]{1,0:T(8,128)}) %all-reduce.8.cloned.1.call-update) | async-done | bytes 524304 | tf_op jit(solution)/shard_map/psum | solution.py:85
  223.7 3.2 %fusion.18 = f32[1,512,128]{1,2,0:T(8,128)S(1)} fusion(f32[1,2,1024,512]{3,2,1,0:T(8,128)} %param.7, f32[1024,128]{1,0:T(8,128)S(1)} %copy-done.1, f32[1024,128]{1,0:T(8,128)} %all-reduce.8.cloned.1.call-done), kind=kOutput, calls=%fused_computation.17 | convolution fusion | flops 805437440 | bytes 3407872 | tf_op jit(solution)/shard_map/dot_general | solution.py:87
  226.9 1.0 copy.7
  (17 shorter events, 0.1 us)
Async XLA Ops:
  6.5 122.2 %all-reduce.4.cloned.1.call-start = ((), (), s32[]{:S(2)}) async-start(), calls=%async_computation.1 | async-start | bytes 1048576 | tf_op jit(solution)/shard_map/psum | solution.py:32
  6.5 18.2 %collective-permute-start = (f32[2,64,1024]{2,1,0:T(8,128)}, f32[2,64,1024]{2,1,0:T(8,128)S(1)}, u32[]{:S(2)}, u32[]{:S(2)}) collective-permute-start(f32[2,64,1024]{2,1,0:T(8,128)} %bitcast.63), channel_id=1, source_target_pairs={{0,1},{1,2},{2,3},{3,4},{4,5},{5,6},{6,7},{7,0},{8,9},{9,10},{10,1... | collective-permute-start | bytes 1572872 | tf_op jit(solution)/shard_map/ppermute | solution.py:46
  24.7 15.8 %collective-permute-start.1 = (f32[2,64,1024]{2,1,0:T(8,128)S(1)}, f32[2,64,1024]{2,1,0:T(8,128)S(1)}, u32[]{:S(2)}, u32[]{:S(2)}) collective-permute-start(f32[2,64,1024]{2,1,0:T(8,128)S(1)} %collective-permute-done), channel_id=1, source_target_pairs={{0,1},{1,2},{2,3},{3,4},{4,5},{5,6},{6,7},{7,0},{8,9},{9,10},{10,1... | collective-permute-start | bytes 1572872 | tf_op jit(solution)/shard_map/ppermute | solution.py:46
  40.5 14.9 %collective-permute-start.2 = (f32[2,64,1024]{2,1,0:T(8,128)S(1)}, f32[2,64,1024]{2,1,0:T(8,128)S(1)}, u32[]{:S(2)}, u32[]{:S(2)}) collective-permute-start(f32[2,64,1024]{2,1,0:T(8,128)S(1)} %collective-permute-done.1), channel_id=1, source_target_pairs={{0,1},{1,2},{2,3},{3,4},{4,5},{5,6},{6,7},{7,0},{8,9},{9,10},{10,1... | collective-permute-start | bytes 1572872 | tf_op jit(solution)/shard_map/ppermute | solution.py:46
  55.4 14.1 %collective-permute-start.3 = (f32[2,64,1024]{2,1,0:T(8,128)S(1)}, f32[2,64,1024]{2,1,0:T(8,128)S(1)}, u32[]{:S(2)}, u32[]{:S(2)}) collective-permute-start(f32[2,64,1024]{2,1,0:T(8,128)S(1)} %collective-permute-done.2), channel_id=1, source_target_pairs={{0,1},{1,2},{2,3},{3,4},{4,5},{5,6},{6,7},{7,0},{8,9},{9,10},{10,1... | collective-permute-start | bytes 1572872 | tf_op jit(solution)/shard_map/ppermute | solution.py:46
  69.5 13.2 %collective-permute-start.4 = (f32[2,64,1024]{2,1,0:T(8,128)S(1)}, f32[2,64,1024]{2,1,0:T(8,128)S(1)}, u32[]{:S(2)}, u32[]{:S(2)}) collective-permute-start(f32[2,64,1024]{2,1,0:T(8,128)S(1)} %collective-permute-done.3), channel_id=1, source_target_pairs={{0,1},{1,2},{2,3},{3,4},{4,5},{5,6},{6,7},{7,0},{8,9},{9,10},{10,1... | collective-permute-start | bytes 1572872 | tf_op jit(solution)/shard_map/ppermute | solution.py:46
  82.7 12.5 %collective-permute-start.5 = (f32[2,64,1024]{2,1,0:T(8,128)S(1)}, f32[2,64,1024]{2,1,0:T(8,128)}, u32[]{:S(2)}, u32[]{:S(2)}) collective-permute-start(f32[2,64,1024]{2,1,0:T(8,128)S(1)} %collective-permute-done.4), channel_id=1, source_target_pairs={{0,1},{1,2},{2,3},{3,4},{4,5},{5,6},{6,7},{7,0},{8,9},{9,10},{10,1... | collective-permute-start | bytes 1572872 | tf_op jit(solution)/shard_map/ppermute | solution.py:46
  95.2 13.0 %collective-permute-start.6 = (f32[2,64,1024]{2,1,0:T(8,128)}, f32[2,64,1024]{2,1,0:T(8,128)}, u32[]{:S(2)}, u32[]{:S(2)}) collective-permute-start(f32[2,64,1024]{2,1,0:T(8,128)} %collective-permute-done.5), channel_id=1, source_target_pairs={{0,1},{1,2},{2,3},{3,4},{4,5},{5,6},{6,7},{7,0},{8,9},{9,10},{10,1... | collective-permute-start | bytes 1572872 | tf_op jit(solution)/shard_map/ppermute | solution.py:46
  99.4 45.2 %reduce-scatter.2.cloned.1.call-start = ((), (), s32[]{:S(2)}) async-start(), calls=%async_computation.2 | async-start | bytes 786432 | tf_op jit(solution)/shard_map/reduce_scatter | solution.py:19
  103.2 12.9 %copy-start = (f32[1,2,64,1024]{3,2,1,0:T(8,128)S(1)}, f32[1,2,64,1024]{3,2,1,0:T(8,128)}, u32[]{:S(2)}) copy-start(f32[1,2,64,1024]{3,2,1,0:T(8,128)} %param.5) | copy-start | bytes 1572868
  121.4 23.1 %copy-start.2 = (f32[1,2,512,128]{3,2,1,0:T(8,128)S(1)}, f32[1,2,512,128]{3,2,1,0:T(8,128)}, u32[]{:S(2)}) copy-start(f32[1,2,512,128]{3,2,1,0:T(8,128)} %param.4) | copy-start | bytes 1572868
  136.5 42.8 %all-reduce.6.cloned.1.call-start = ((), (), s32[]{:S(2)}) async-start(), calls=%async_computation.3 | async-start | bytes 1048576 | tf_op jit(solution)/shard_map/psum | solution.py:32
  149.4 74.3 %copy-start.1 = (f32[1024,128]{1,0:T(8,128)S(1)}, f32[1024,128]{1,0:T(8,128)}, u32[]{:S(2)}) copy-start(f32[1024,128]{1,0:T(8,128)} %all-reduce.4.cloned.1.call-done) | copy-start | bytes 1572868
  149.4 74.3 %all-reduce.8.cloned.1.call-start = ((), (), s32[]{:S(2)}) async-start(), calls=%async_computation.4 | async-start | bytes 1048576 | tf_op jit(solution)/shard_map/psum | solution.py:85
Sparse Core Ops, SparseCore 0:
  99.5 29.2 all-reduce.3
  136.6 7.9 reduce-scatter.1
  149.5 29.7 all-reduce.5
  195.0 28.6 all-reduce.7
